TPU v7x, 32 devices: a whole 2x2x4 slice. The times are simulated.
32 devices in a mesh: row: 4 (over y, core), col: 8 (over z, x).
Axes of the slice: x: 2, y: 2, z: 4, core: 2. Of those that a mesh axis runs over, the one named last changes fastest.
Arguments:
- schur_matrix: float32 [16384, 16384], P('row', 'col'), may hold values from -3 to 7
- newton_rhs: float32 [16384], P('row'), may hold values from -6 to 6
Outputs:
- reduced_matrix: float32 [16384, 16384], P('row', 'col')
- reduced_rhs: float32 [16384], P('row')
All inputs are finite; a program needn't handle non-finite values.
Results may differ from a plain program's by a relative error of at most 0.0001.
Values sent between devices are 32-bit elements; how exact they have to be, the bound alone decides.
No kernel may reach another device: no remote copies, remote signals or barrier semaphores. Data moves between devices by JAX's collectives and lax.ppermute only.
A program may use at most 128 MiB of HBM per device.

v0:
```python
import jax
import jax.numpy as jnp
from jax import lax
from jax.sharding import PartitionSpec as P

NB = 512


def broadcast(value, axis, source):
    kept = jnp.where(lax.axis_index(axis) == source, value, 0).astype(value.dtype)
    return lax.psum(kept, axis)


def precise_dot(left, right):
    return jnp.dot(left, right, precision=lax.Precision.HIGHEST, preferred_element_type=jnp.float32)


def invert_pivot(pivot_block, holds_pivot):
    identity = jnp.eye(pivot_block.shape[0], dtype=jnp.float32)
    diag_vals = jnp.where(holds_pivot, jnp.diagonal(pivot_block), 1.0)
    inv_diag = 1.0 / diag_vals
    first_iter = inv_diag[:, None] * (2.0 * identity - pivot_block * inv_diag[None, :])
    return precise_dot(first_iter, 2.0 * identity - precise_dot(pivot_block, first_iter))


def shards(schur_matrix, newton_rhs):
    row_count = lax.axis_size("row")
    col_count = lax.axis_size("col")
    own_row = lax.axis_index("row")
    own_col = lax.axis_index("col")
    local_rows, local_cols = schur_matrix.shape
    row_block = jnp.arange(local_rows, dtype=jnp.int32) // NB * row_count + own_row
    col_block = jnp.arange(local_cols, dtype=jnp.int32) // NB * col_count + own_col
    matrix_now = schur_matrix
    rhs_now = newton_rhs
    root_row = 0 % row_count
    lead_row = 0 // row_count * NB
    root_col = 0 % col_count
    lead_col = 0 // col_count * NB
    live_rows = row_block > 0
    live_mask = live_rows[:, None] & (col_block > 0)[None, :]
    col_panel = broadcast(matrix_now[:, lead_col : lead_col + NB], "col", root_col)
    pivot_block = col_panel[lead_row : lead_row + NB, :]
    inverse = invert_pivot(pivot_block, own_row == root_row)
    product = precise_dot(inverse, matrix_now[lead_row : lead_row + NB, :])
    solved = precise_dot(inverse, rhs_now[lead_row : lead_row + NB])
    product, solved = (broadcast(product, "row", root_row), broadcast(solved, "row", root_row))
    update = precise_dot(col_panel, product)
    rhs_shift = precise_dot(col_panel, solved)
    matrix_now = matrix_now - jnp.where(live_mask, update, 0.0)
    rhs_now = rhs_now - jnp.where(live_rows, rhs_shift, 0.0)
    return (matrix_now, rhs_now)


def solution(mesh):
    return jax.shard_map(
        shards,
        mesh=mesh,
        in_specs=(P("row", "col"), P("row")),
        out_specs=(P("row", "col"), P("row")),
        check_vma=False,
    )
```

profile of v0, /device:TPU:0, one launch (start us, length us, event | category | flops | bytes accessed | tf_op | source)
XLA Modules:
  0.0 465.4 jit_solution(12003061219521151219)
XLA Ops:
  7.2 0.0 all-reduce.3.cloned.1.call-start
  7.2 7.8 %slice_select_fusion = f32[4096,512]{1,0:T(8,128)} fusion(f32[4096,2048]{1,0:T(8,128)} %param.2, pred[]{:T(512)S(6)} %eq.13), kind=kLoop, calls=%fused_computation.2 | loop fusion | flops 2097152 | bytes 16777216 | tf_op jit(solution)/shard_map/jit(_where)/select_n | solution.py:10
  15.0 0.0 all-reduce.3.cloned.1.call-update
  15.1 0.0 all-reduce.5.cloned.1.call-start
  15.1 272.8 %all-reduce.3.cloned.1.call-done = f32[4096,512]{1,0:T(8,128)} async-done(((f32[4096,512]{1,0:T(8,128)}), f32[4096,512]{1,0:T(8,128)}) %all-reduce.3.cloned.1.call-update) | async-done | bytes 8388624 | tf_op jit(solution)/shard_map/psum | solution.py:11
  287.9 1.3 slice.18
  289.2 4.5 gather_fusion
  293.8 3.6 select_subtract_fusion.1
  297.4 3.2 fusion.6
  300.5 0.0 slice-start
  300.6 10.1 %fusion.2 = f32[512,2048]{1,0:T(8,128)} fusion(f32[512,512]{1,0:T(8,128)S(1)} %fusion.6, f32[4096,2048]{1,0:T(8,128)} %param.2, pred[]{:T(512)S(6)} %eq.14), kind=kOutput, calls=%fused_computation.5 | convolution fusion | flops 6443499520 | bytes 9437185 | tf_op jit(solution)/shard_map/dot_general | solution.py:15
  310.6 0.0 copy-start
  310.6 0.0 all-reduce.5.cloned.1.call-update
  310.7 0.0 slice-done
  310.7 1.0 fusion.35
  311.7 6.6 %psum.23 = f32[512]{0:T(512)S(1)} all-reduce(f32[512]{0:T(512)S(1)} %broadcast_select_fusion), channel_id=1, replica_groups=mesh['row'=4,'col'=8] {'row'}, use_global_device_ids=true, to_apply=%region_2.3 | all-reduce | flops 512 | bytes 4096 | tf_op jit(solution)/shard_map/psum | solution.py:11
  318.3 9.4 %fusion.36 = f32[1,4096]{1,0:T(1,128)S(1)} fusion(f32[4096,512]{1,0:T(8,128)} %all-reduce.3.cloned.1.call-done, f32[512,1]{0,1:T(1,128)S(1)} %bitcast.17), kind=kOutput, calls=%fused_computation.50 | convolution fusion | flops 25165824 | bytes 8407040 | tf_op jit(solution)/shard_map/dot_general | solution.py:15
  327.7 0.0 copy-done
  327.7 0.6 select_subtract_fusion.3
  328.3 67.1 %all-reduce.5.cloned.1.call-done = f32[512,2048]{1,0:T(8,128)} async-done(((f32[512,2048]{1,0:T(8,128)}), f32[512,2048]{1,0:T(8,128)}) %all-reduce.5.cloned.1.call-update) | async-done | bytes 4194320 | tf_op jit(solution)/shard_map/psum | solution.py:11
  395.4 63.1 %select_subtract_fusion = f32[4096,2048]{1,0:T(8,128)} fusion(f32[4096,2048]{1,0:T(8,128)} %param.2, pred[2048]{0:T(1024)(128)(4,1)S(1)} %fusion.25, pred[4096]{0:T(1024)(128)(4,1)S(1)} %fusion.19, f32[4096,512]{1,0:T(8,128)} %all-reduce.3.cloned.1.call-done, f32[512,2048]{1,0:T(8,128)} %all-reduce.5.cloned.1.call-done), kind=kOutput, calls=%fused_computation.1 | convolution fusion | flops 51564773376 | bytes 79697920 | tf_op jit(solution)/shard_map/dot_general | solution.py:15
  (5 shorter events, 0.0 us)
Async XLA Ops:
  7.2 280.8 %all-reduce.3.cloned.1.call-start = ((), (), s32[]{:S(2)}) async-start(), calls=%async_computation | async-start | bytes 16777216 | tf_op jit(solution)/shard_map/psum | solution.py:11
  15.1 380.4 %all-reduce.5.cloned.1.call-start = ((), (), s32[]{:S(2)}) async-start(), calls=%async_computation.1 | async-start | bytes 8388608 | tf_op jit(solution)/shard_map/psum | solution.py:11
  300.5 10.1 %slice-start = ((f32[4096]{0:T(1024)}), f32[512]{0:T(512)S(1)}, s32[]{:S(2)}) async-start(f32[4096]{0:T(1024)} %param.3), calls=%async_computation.2 | async-start | bytes 4096 | tf_op jit(solution)/shard_map/slice | solution.py:46
  310.6 17.1 %copy-start = (f32[4096]{0:T(1024)S(1)}, f32[4096]{0:T(1024)}, u32[]{:S(2)}) copy-start(f32[4096]{0:T(1024)} %param.3) | copy-start | bytes 49156
Sparse Core Ops, SparseCore 0:
  15.2 272.7 all-reduce.2
  310.8 84.5 all-reduce.4
where the time goes:
time: 466 us; the launch traced here: 465 us
  waiting for transfers between devices  340 us (73%)
  matrix products  90.4 us (19%)
  between operations  14.1 us (3%)
  other arithmetic  8.47 us (2%)
  blocking collectives  6.58 us (1%)
  local copies, waits for them, and re-layouts  5.83 us (1%)
    psum x2, waiting for transfers between devices, broadcast(): return lax.psum(kept, axis)  340 us
    dot_general x6, matrix products, precise_dot(): jnp.dot(left, right, precision=lax.Precision.HIGHEST, preferred_element_t...  90.4 us
  transfers between devices with their start and end apart: 2, of which 2 were waited for; matrix products, arithmetic and copies ran while one was open for 2% of the time, Pallas kernels for 0%

commit v1 on v0

v1 whole, which is shorter than its diff:
```python
import jax
import jax.numpy as jnp
from jax import lax
from jax.experimental import pallas as pl
from jax.experimental.pallas import tpu as pltpu
from jax.sharding import PartitionSpec as P


NB = 512
F32, BF16 = jnp.float32, jnp.bfloat16
ANY = pl.BlockSpec(memory_space=pl.ANY)
VMEM = pl.BlockSpec(memory_space=pltpu.VMEM)


def barrier(value, ties):
    return lax.optimization_barrier((value, *ties))[0] if ties else value


def dot(left, right):
    return jnp.dot(left, right, preferred_element_type=F32)


def precise_dot(left, right, dims=(((1,), (0,)), ((), ()))):
    return lax.dot_general(left, right, dims, precision=lax.Precision.HIGHEST, preferred_element_type=F32)


def split_dot(left, right):
    return dot(left[0], right[0]) + dot(left[0], right[1]) + dot(left[1], right[0])


def halves(value):
    high = value.astype(BF16)
    return high, (value - high.astype(F32)).astype(BF16)


def solve_kernel(place, pivot_ref, matrix, *refs):
    *received, high_ref, low_ref, solved_ref, strip, sem = refs
    nb, local_cols = strip.shape
    sources = [matrix.at[:nb, :], *received]
    for at, source in enumerate(sources):

        @pl.when(place[0] == at)
        def _():
            pltpu.make_async_copy(source, strip, sem).start()

    block = pivot_ref[:nb, :]
    on_diag = lax.broadcasted_iota(jnp.int32, (nb, nb), 0) == lax.broadcasted_iota(jnp.int32, (nb, nb), 1)
    diag = jnp.where(on_diag, block, 0.0)
    inv_row = 1.0 / jnp.sum(diag, axis=0, keepdims=True)
    inv_col = 1.0 / jnp.sum(diag, axis=1, keepdims=True)
    twice = jnp.where(on_diag, 2.0, 0.0)
    first_iter = inv_col * (twice - block * inv_row)
    inverse = split_dot(halves(first_iter), halves(twice - split_dot(halves(block), halves(first_iter))))
    solved_ref[...] = precise_dot(pivot_ref[nb:, :], inverse, (((1,), (1,)), ((), ())))
    inv_parts = halves(inverse)
    pltpu.make_async_copy(sources[0], strip, sem).wait()

    @pl.loop(0, local_cols // nb)
    def _(at):
        cols = pl.ds(pl.multiple_of(at * nb, nb), nb)
        product = split_dot(inv_parts, halves(strip[:, cols]))
        product = jnp.where((place[1] == 0) & (at == 0), 0.0, product)
        high_ref[:, cols], low_ref[:, cols] = halves(product)


def update_kernel(count, tile, rhs, high_ref, low_ref, solved_ref, *refs):
    sources = refs[:count]
    out_tile, out_rhs, panel, sems = refs[-4:]
    nb = panel.shape[1]
    at = pl.program_id(0)
    slot = lax.rem(at, 2)

    def fetch(step):
        for which, source in enumerate(sources):

            @pl.when(step == which)
            def _():
                pltpu.make_async_copy(source, panel.at[which % 2], sems.at[which % 2]).start()

    @pl.when(at == 0)
    def _():
        fetch(0)

    pltpu.make_async_copy(sources[0], panel.at[slot], sems.at[slot]).wait()
    fetch(at + 1)
    value = panel[slot]
    out_tile[...] = tile[...] - split_dot(halves(value), (high_ref[...], low_ref[...]))
    terms = value * solved_ref[0:1, :]
    folded = terms[:, :128]
    for low_col in range(128, nb, 128):
        folded = folded + terms[:, low_col : low_col + 128]
    out_rhs[...] = rhs[...] - jnp.sum(folded.T, axis=0, keepdims=True)


def solve(place, pivot, matrix, received):
    local_cols = matrix.shape[1]
    nb = pivot.shape[1]
    return pl.pallas_call(
        solve_kernel,
        grid_spec=pltpu.PrefetchScalarGridSpec(
            num_scalar_prefetch=1,
            grid=(),
            in_specs=[VMEM, ANY, *[ANY] * len(received)],
            out_specs=[VMEM] * 3,
            scratch_shapes=[pltpu.VMEM((nb, local_cols), F32), pltpu.SemaphoreType.DMA],
        ),
        out_shape=[jax.ShapeDtypeStruct((nb, local_cols), BF16)] * 2 + [jax.ShapeDtypeStruct((8, nb), F32)],
        compiler_params=pltpu.CompilerParams(vmem_limit_bytes=24 * 2**20),
        cost_estimate=pl.CostEstimate(flops=6 * nb * nb * local_cols + 24 * nb**3, bytes_accessed=8 * nb * local_cols, transcendentals=0),
        name="solve",
    )(place, pivot, matrix, *received)


def update(start, matrix, rhs, factors, panels, before):
    _, local_cols = matrix.shape
    nb, count = factors[0].shape[0], len(panels)
    at_tile = pl.BlockSpec((nb, local_cols), lambda at: (start + at, 0))
    at_rhs = pl.BlockSpec((1, nb), lambda at: (0, start + at))
    factor = pl.BlockSpec((nb, local_cols), lambda at: (0, 0), pipeline_mode=pl.Buffered(1))
    operands = [matrix, rhs, *factors, *panels, *before]
    return pl.pallas_call(
        lambda *refs: update_kernel(count, *refs),
        grid=(count,),
        in_specs=[at_tile, at_rhs, factor, factor, VMEM, *[ANY] * (count + len(before))],
        out_specs=[at_tile, at_rhs],
        scratch_shapes=[pltpu.VMEM((2, nb, nb), F32), pltpu.SemaphoreType.DMA((2,))],
        out_shape=[jax.ShapeDtypeStruct(matrix.shape, F32), jax.ShapeDtypeStruct(rhs.shape, F32)],
        input_output_aliases={len(operands) - 2 + at: at for at in range(len(before))},
        compiler_params=pltpu.CompilerParams(dimension_semantics=("arbitrary",), vmem_limit_bytes=32 * 2**20),
        cost_estimate=pl.CostEstimate(flops=6 * count * nb * nb * local_cols, bytes_accessed=8 * count * nb * local_cols, transcendentals=0),
        name="update",
    )(*operands)


def fan_out(source, low, high):
    if low >= high:
        return []
    mid = (low + high) // 2
    return [(0, source, mid)] + [(at + 1, a, b) for at, a, b in fan_out(mid, low, mid) + fan_out(mid, mid + 1, high)]


def parent(row):
    return row & (row - 1)


def plan(count, stages, row_count):
    last = max(at for at, _, _ in stages)
    levels = {row: bin(row).count("1") for row in range(1, row_count)}
    late = max(levels.values())
    launches = [(name, at) for at in range(count) for name in ("first", "lower")]
    order = launches[:8] + [("onward", 0)]
    launches = launches[8:]
    side_work = {0: [("strip", row) for row in levels if levels[row] == 1]}
    for level in range(1, late + 1):
        side_work[last + 2 * level] = [(name, row) for name in ("strip", "pivot") for row in levels if levels[row] == level and (name == "pivot" or level > 1)]
    side_work.setdefault(max(count - 1, last + 2 * late + 1), []).append(("solve", 0))
    early = [max(count - 6, 0), max(count - 2, 0)]
    for step in range(count + last + 2):
        for stage in range(1, last + 1):
            pair = step - stage + 1
            if 0 <= pair <= count:
                order += [("spread", pair, b) for s, _, b in stages if s == stage]
        if 0 <= step - last <= count:
            order.append(("cross", step - last))
        if 0 <= step - last - 1 < count:
            order.append(("close", step - last - 1))
        if step + 1 < count:
            order.append(("onward", step + 1))
        if step > 0:
            order += launches[:4]
            launches = launches[4:]
        order += side_work.pop(step, [])
        if step >= count and ("solve", 0) in order and early:
            order.append(("update", early.pop(0)))
    order += launches + [work for at in sorted(side_work) for work in side_work[at]]
    starts = [0, *[step[1] for step in order if step[0] == "update"], count]
    groups = list(zip(sorted({*starts}), sorted({*starts})[1:]))
    ended = {high: low for low, high in groups}
    order = [("update", ended[step[1]], step[1]) if step[0] == "update" else step for step in order if step[0] != "update" or step[1] in ended]
    return order + [("update", ended[count], count)]


def shards(order, stages, schur_matrix, newton_rhs):
    row_count, col_count = lax.axis_size("row"), lax.axis_size("col")
    own_row, own_col = lax.axis_index("row"), lax.axis_index("col")
    local_rows, _ = schur_matrix.shape
    depth = col_count // 2
    line, side = own_col // 2, own_col % 2
    count, half = local_rows // NB, NB // 2
    last = max(at for at, _, _ in stages)
    mid = stages[0][2]

    def link(value, *pairs):
        return lax.ppermute(value, "col", [(a * 2 + i, b * 2 + j) for (a, i), (b, j) in pairs])

    def down(value, row):
        above = parent(row)
        if row - above > 1:
            return lax.ppermute(value, "row", [(above, row)])
        return lax.ppermute(value, "row", [(at, at ^ 1) for at in range(row_count)])

    def choose(options):
        return jnp.where(place[2] == 0, options[0], jnp.where(place[2] == 1, options[1], jnp.where(side == 0, options[2], options[3])))

    def cut(source, low, high):
        return list(lax.optimization_barrier([source[at * half : (at + 1) * half, :NB] for at in range(low, high)]))

    pieces = cut(schur_matrix, 0, 4)
    later = barrier(schur_matrix, pieces)
    pieces += cut(later, 4, 8)
    later = barrier(later, pieces[4:])
    strip = lax.optimization_barrier(later[:NB, :])
    pieces += cut(barrier(later, [strip]), 8, 2 * count)
    place = jnp.stack([own_row, own_col, jnp.where(own_col < 2, own_col, 2 + side)]).astype(jnp.int32)
    rhs = newton_rhs.reshape(1, local_rows)

    sides = {at: [i for i, ok in ((0, at < count), (1, at > 0)) if ok] for at in range(count + 1)}
    sources = {b: (a, stage) for stage, a, b in stages}
    first, lower, onward, spread, crossed, closed = {}, {}, {}, {}, {}, {}
    columns, panels, strips, pivots, factors, done = {}, {}, {0: strip}, {}, None, ()

    def column(pair, stage):
        if (pair, stage) not in columns:
            if stage == 1:
                a, b = onward.get(pair - 1), lower.get(pair)
                columns[pair, 1] = b if a is None else a if b is None else jnp.where(side == 0, b, a)
            else:
                value = column(pair, stage - 1)
                for s, _, b in stages:
                    if s == stage - 1:
                        value = jnp.where(line == b, spread[pair, b], value)
                columns[pair, stage] = value
        return columns[pair, stage]

    def panel(section):
        if section not in panels:
            own = barrier(schur_matrix, [closed[section]])[section * NB : (section + 1) * NB, :NB]
            upper = [own[:half], first[section], crossed[section + 1], column(section + 1, last + 1)]
            under = [own[half:], closed[section], column(section, last + 1), crossed[section]]
            panels[section] = jnp.concatenate([choose(upper), choose(under)])
        return panels[section]

    for step in order:
        name, at = step[:2]
        if name == "pivot" and 0 not in pivots:
            pivots[0] = jnp.concatenate([panel(0), jnp.broadcast_to(newton_rhs[None, :NB], (8, NB))])
        if name == "solve":
            block = pivots[0]
            for row in range(1, row_count):
                block = jnp.where(own_row == row, pivots[row], block)
        if name == "first":
            first[at] = link(pieces[2 * at], ((0, 0), (0, 1)))
        elif name == "lower":
            lower[at] = link(pieces[2 * at + 1], ((0, 0), (mid, 0)))
        elif name == "onward":
            onward[at] = link(first[at], ((0, 1), (mid, 1)))
        elif name == "spread":
            source, stage = sources[step[2]]
            spread[at, step[2]] = link(column(at, stage), *[((source, i), (step[2], i)) for i in sides[at]])
        elif name == "cross":
            crossed[at] = link(column(at, last + 1), *[((k, i), (k, 1 - i)) for k in range(1, depth) for i in sides[at]])
        elif name == "close":
            closed[at] = link(crossed[at], ((1, 1), (0, 1)))
        elif name == "strip":
            strips[at] = down(strips[parent(at)], at)
        elif name == "pivot":
            pivots[at] = down(pivots[parent(at)], at)
        elif name == "solve":
            factors = solve(place, block, schur_matrix, [strips[row] for row in range(1, row_count)])
        else:
            group = [panel(section) for section in range(at, step[2])]
            if at == 0:
                group[0] = jnp.where(own_row == 0, 0.0, group[0])
            done = update(at, schur_matrix, rhs, factors, group, done)
    return done[0], done[1].reshape(local_rows)


def solution(mesh):
    row_count, col_count = mesh.shape["row"], mesh.shape["col"]
    stages = fan_out(0, 1, col_count // 2)

    def program(schur_matrix, newton_rhs):
        order = plan(schur_matrix.shape[0] // row_count // NB, stages, row_count)

        def body(*args):
            return shards(order, stages, *args)

        step = jax.shard_map(
            body,
            mesh=mesh,
            in_specs=(P("row", "col"), P("row")),
            out_specs=(P("row", "col"), P("row")),
            check_vma=False,
        )
        return step(schur_matrix, newton_rhs)

    return program
```

time: 466 us -> 465 us (level)
  the two profiles are of different devices: /device:TPU:0 before, /device:TPU:7 now
where the time goes in v1:
time: 465 us; the launch traced here: 463 us
  waiting for transfers between devices  273 us (59%)
  starting transfers between devices  102 us (22%)
  Pallas kernels  50.7 us (11%)
  other arithmetic  20.4 us (4%)
  local copies, waits for them, and re-layouts  13.9 us (3%)
    ppermute x59, waiting for transfers between devices, link(): lax.ppermute(value, 'col', [(a * 2 + i, b * 2 + j) for (a, i), (b, j) in...  273 us
    ppermute x59, starting transfers between devices, link(): lax.ppermute(value, 'col', [(a * 2 + i, b * 2 + j) for (a, i), (b, j) in...  73.5 us
    pallas_call x3, Pallas kernels, update(): pl.pallas_call(lambda *refs: update_kernel(count, *refs), grid=(count,),...  41.4 us
    ppermute x4, starting transfers between devices, down(): return lax.ppermute(value, 'row', [(at, at ^ 1) for at in range(row_count)])  25.4 us
    select_n x5, other arithmetic, choose(): jnp.where(place[2] == 0, options[0], jnp.where(place[2] == 1, options[1],...  11.8 us
    pallas_call x1, Pallas kernels, solve(): pl.pallas_call(solve_kernel, grid_spec=pltpu.PrefetchScalarGridSpec(num_s...  9.35 us
  transfers between devices with their start and end apart: 65, of which 23 were waited for; matrix products, arithmetic and copies ran while one was open for 6% of the time, Pallas kernels for 0%

profile of v1, /device:TPU:7, one launch (start us, length us, event | category | flops | bytes accessed | tf_op | source)
XLA Modules:
  0.0 463.0 jit_solution(12743368610337289768)
XLA Ops:
  10.8 4.7 %slice.137 = f32[512,2048]{1,0:T(8,128)} slice(f32[4096,2048]{1,0:T(8,128)} %refs_0_.5), slice={[0:512], [0:2048]} | slice | bytes 8388608 | tf_op jit(solution)/shard_map/slice | solution.py:212
  15.5 4.7 %collective-permute-done.5 = f32[256,512]{1,0:T(8,128)S(1)} collective-permute-done((f32[256,512]{1,0:T(8,128)S(1)}, f32[256,512]{1,0:T(8,128)S(1)}, u32[]{:S(2)}, u32[]{:S(2)}) %collective-permute-start.5) | collective-permute-done | bytes 524320 | tf_op jit(solution)/shard_map/ppermute | solution.py:194
  25.2 6.3 %collective-permute-done.37 = f32[256,512]{1,0:T(8,128)S(1)} collective-permute-done((f32[256,512]{1,0:T(8,128)S(1)}, f32[256,512]{1,0:T(8,128)S(1)}, u32[]{:S(2)}, u32[]{:S(2)}) %collective-permute-start.37) | collective-permute-done | bytes 524320 | tf_op jit(solution)/shard_map/ppermute | solution.py:194
  32.2 10.5 %collective-permute-done.43 = f32[256,512]{1,0:T(8,128)S(1)} collective-permute-done((f32[256,512]{1,0:T(8,128)S(1)}, f32[256,512]{1,0:T(8,128)S(1)}, u32[]{:S(2)}, u32[]{:S(2)}) %collective-permute-start.43) | collective-permute-done | bytes 524320 | tf_op jit(solution)/shard_map/ppermute | solution.py:194
  45.3 8.6 %collective-permute-done.50 = f32[256,512]{1,0:T(8,128)S(1)} collective-permute-done((f32[256,512]{1,0:T(8,128)S(1)}, f32[256,512]{1,0:T(8,128)S(1)}, u32[]{:S(2)}, u32[]{:S(2)}) %collective-permute-start.50) | collective-permute-done | bytes 524320 | tf_op jit(solution)/shard_map/ppermute | solution.py:194
  56.8 8.4 %collective-permute-done.18 = f32[256,512]{1,0:T(8,128)S(1)} collective-permute-done((f32[256,512]{1,0:T(8,128)S(1)}, f32[256,512]{1,0:T(8,128)S(1)}, u32[]{:S(2)}, u32[]{:S(2)}) %collective-permute-start.18) | collective-permute-done | bytes 524320 | tf_op jit(solution)/shard_map/ppermute | solution.py:194
  66.5 9.9 %collective-permute-done.24 = f32[256,512]{1,0:T(8,128)S(1)} collective-permute-done((f32[256,512]{1,0:T(8,128)S(1)}, f32[256,512]{1,0:T(8,128)S(1)}, u32[]{:S(2)}, u32[]{:S(2)}) %collective-permute-start.24) | collective-permute-done | bytes 524320 | tf_op jit(solution)/shard_map/ppermute | solution.py:194
  78.6 9.1 %collective-permute-done.31 = f32[256,512]{1,0:T(8,128)S(1)} collective-permute-done((f32[256,512]{1,0:T(8,128)S(1)}, f32[256,512]{1,0:T(8,128)S(1)}, u32[]{:S(2)}, u32[]{:S(2)}) %collective-permute-start.31) | collective-permute-done | bytes 524320 | tf_op jit(solution)/shard_map/ppermute | solution.py:194
  91.2 7.6 %collective-permute-done.57 = f32[256,512]{1,0:T(8,128)S(1)} collective-permute-done((f32[256,512]{1,0:T(8,128)S(1)}, f32[256,512]{1,0:T(8,128)S(1)}, u32[]{:S(2)}, u32[]{:S(2)}) %collective-permute-start.57) | collective-permute-done | bytes 524320 | tf_op jit(solution)/shard_map/ppermute | solution.py:194
  111.9 5.1 %collective-permute-start.26 = (f32[256,512]{1,0:T(8,128)S(1)}, f32[256,512]{1,0:T(8,128)S(1)}, u32[]{:S(2)}, u32[]{:S(2)}) collective-permute-start(f32[256,512]{1,0:T(8,128)S(1)} %collective-permute-done.24), channel_id=1, source_target_pairs={{1,5},{9,13},{17,21},{25,29}} | collective-permute-start | bytes 1572872 | tf_op jit(solution)/shard_map/ppermute | solution.py:194
  117.0 6.1 %collective-permute-done.45 = f32[256,512]{1,0:T(8,128)} collective-permute-done((f32[256,512]{1,0:T(8,128)S(1)}, f32[256,512]{1,0:T(8,128)}, u32[]{:S(2)}, u32[]{:S(2)}) %collective-permute-start.45) | collective-permute-done | bytes 524320 | tf_op jit(solution)/shard_map/ppermute | solution.py:194
  123.1 5.1 %collective-permute-start.32 = (f32[256,512]{1,0:T(8,128)S(1)}, f32[256,512]{1,0:T(8,128)S(1)}, u32[]{:S(2)}, u32[]{:S(2)}) collective-permute-start(f32[256,512]{1,0:T(8,128)S(1)} %copy-done.27), channel_id=1, source_target_pairs={{1,5},{9,13},{17,21},{25,29}} | collective-permute-start | bytes 1572872 | tf_op jit(solution)/shard_map/ppermute | solution.py:194
  129.4 4.9 %collective-permute-done.52 = f32[256,512]{1,0:T(8,128)S(1)} collective-permute-done((f32[256,512]{1,0:T(8,128)S(1)}, f32[256,512]{1,0:T(8,128)S(1)}, u32[]{:S(2)}, u32[]{:S(2)}) %collective-permute-start.52) | collective-permute-done | bytes 524320 | tf_op jit(solution)/shard_map/ppermute | solution.py:194
  134.4 5.0 %collective-permute-start.59 = (f32[256,512]{1,0:T(8,128)S(1)}, f32[256,512]{1,0:T(8,128)S(1)}, u32[]{:S(2)}, u32[]{:S(2)}) collective-permute-start(f32[256,512]{1,0:T(8,128)S(1)} %copy-done.24), channel_id=1, source_target_pairs={{1,5},{9,13},{17,21},{25,29}} | collective-permute-start | bytes 1572872 | tf_op jit(solution)/shard_map/ppermute | solution.py:194
  140.5 5.0 %collective-permute-done.19 = f32[256,512]{1,0:T(8,128)S(1)} collective-permute-done((f32[256,512]{1,0:T(8,128)S(1)}, f32[256,512]{1,0:T(8,128)S(1)}, u32[]{:S(2)}, u32[]{:S(2)}) %collective-permute-start.19) | collective-permute-done | bytes 524320 | tf_op jit(solution)/shard_map/ppermute | solution.py:194
  146.3 10.5 %collective-permute-done.26 = f32[256,512]{1,0:T(8,128)S(1)} collective-permute-done((f32[256,512]{1,0:T(8,128)S(1)}, f32[256,512]{1,0:T(8,128)S(1)}, u32[]{:S(2)}, u32[]{:S(2)}) %collective-permute-start.26) | collective-permute-done | bytes 524320 | tf_op jit(solution)/shard_map/ppermute | solution.py:194
  157.5 10.5 %collective-permute-done.32 = f32[256,512]{1,0:T(8,128)S(1)} collective-permute-done((f32[256,512]{1,0:T(8,128)S(1)}, f32[256,512]{1,0:T(8,128)S(1)}, u32[]{:S(2)}, u32[]{:S(2)}) %collective-permute-start.32) | collective-permute-done | bytes 524320 | tf_op jit(solution)/shard_map/ppermute | solution.py:194
  169.9 9.4 %collective-permute-done.59 = f32[256,512]{1,0:T(8,128)S(1)} collective-permute-done((f32[256,512]{1,0:T(8,128)S(1)}, f32[256,512]{1,0:T(8,128)S(1)}, u32[]{:S(2)}, u32[]{:S(2)}) %collective-permute-start.59) | collective-permute-done | bytes 524320 | tf_op jit(solution)/shard_map/ppermute | solution.py:194
  195.0 66.5 %collective-permute-done.4 = f32[256,512]{1,0:T(8,128)S(1)} collective-permute-done((f32[256,512]{1,0:T(8,128)S(1)}, f32[256,512]{1,0:T(8,128)S(1)}, u32[]{:S(2)}, u32[]{:S(2)}) %collective-permute-start.4) | collective-permute-done | bytes 524320 | tf_op jit(solution)/shard_map/ppermute | solution.py:194
  268.1 5.2 %collective-permute-start.14 = (f32[512,2048]{1,0:T(8,128)}, f32[512,2048]{1,0:T(8,128)}, u32[]{:S(2)}, u32[]{:S(2)}) collective-permute-start(f32[512,2048]{1,0:T(8,128)} %slice.137), channel_id=1, source_target_pairs={{0,8},{8,0},{16,24},{24,16},{1,9},{9,1},{17,25},{25,17},{2,10},{10... | collective-permute-start | bytes 12582920 | tf_op jit(solution)/shard_map/ppermute | solution.py:200
  274.6 30.4 %collective-permute-done.64 = f32[256,512]{1,0:T(8,128)S(1)} collective-permute-done((f32[256,512]{1,0:T(8,128)S(1)}, f32[256,512]{1,0:T(8,128)S(1)}, u32[]{:S(2)}, u32[]{:S(2)}) %collective-permute-start.64) | collective-permute-done | bytes 524320 | tf_op jit(solution)/shard_map/ppermute | solution.py:194
  306.3 11.2 %collective-permute-done.42 = f32[256,512]{1,0:T(8,128)S(1)} collective-permute-done((f32[256,512]{1,0:T(8,128)S(1)}, f32[256,512]{1,0:T(8,128)S(1)}, u32[]{:S(2)}, u32[]{:S(2)}) %collective-permute-start.42) | collective-permute-done | bytes 524320 | tf_op jit(solution)/shard_map/ppermute | solution.py:194
  321.1 20.2 %collective-permute-done.49 = f32[256,512]{1,0:T(8,128)} collective-permute-done((f32[256,512]{1,0:T(8,128)}, f32[256,512]{1,0:T(8,128)}, u32[]{:S(2)}, u32[]{:S(2)}) %collective-permute-start.49) | collective-permute-done | bytes 524320 | tf_op jit(solution)/shard_map/ppermute | solution.py:194
  342.0 10.5 %collective-permute-done.23 = f32[256,512]{1,0:T(8,128)} collective-permute-done((f32[256,512]{1,0:T(8,128)}, f32[256,512]{1,0:T(8,128)}, u32[]{:S(2)}, u32[]{:S(2)}) %collective-permute-start.23) | collective-permute-done | bytes 524320 | tf_op jit(solution)/shard_map/ppermute | solution.py:194
  353.9 9.9 %collective-permute-done.30 = f32[256,512]{1,0:T(8,128)} collective-permute-done((f32[256,512]{1,0:T(8,128)S(1)}, f32[256,512]{1,0:T(8,128)}, u32[]{:S(2)}, u32[]{:S(2)}) %collective-permute-start.30) | collective-permute-done | bytes 524320 | tf_op jit(solution)/shard_map/ppermute | solution.py:194
  368.0 6.9 %collective-permute-done.56 = f32[256,512]{1,0:T(8,128)S(1)} collective-permute-done((f32[256,512]{1,0:T(8,128)}, f32[256,512]{1,0:T(8,128)S(1)}, u32[]{:S(2)}, u32[]{:S(2)}) %collective-permute-start.56) | collective-permute-done | bytes 524320 | tf_op jit(solution)/shard_map/ppermute | solution.py:194
  375.0 7.4 %collective-permute-start.13 = (f32[520,512]{1,0:T(8,128)S(1)}, f32[520,512]{1,0:T(8,128)S(1)}, u32[]{:S(2)}, u32[]{:S(2)}) collective-permute-start(f32[520,512]{1,0:T(8,128)S(1)} %pad_maximum_fusion), channel_id=1, source_target_pairs={{0,8},{8,0},{16,24},{24,16},{1,9},{9,1},{17,25},{25,17},{2,10},{10... | collective-permute-start | bytes 3194888 | tf_op jit(solution)/shard_map/ppermute | solution.py:200
  394.3 12.7 %collective-permute-start.12 = (f32[520,512]{1,0:T(8,128)S(1)}, f32[520,512]{1,0:T(8,128)S(1)}, u32[]{:S(2)}, u32[]{:S(2)}) collective-permute-start(f32[520,512]{1,0:T(8,128)S(1)} %collective-permute-done.11), channel_id=1, source_target_pairs={{0,8},{8,0},{16,24},{24,16},{1,9},{9,1},{17,25},{25,17},{2,10},{10... | collective-permute-start | bytes 3194888 | tf_op jit(solution)/shard_map/ppermute | solution.py:200
  412.1 9.4 %solve.1 = (bf16[512,2048]{1,0:T(8,128)(2,1)S(1)}, bf16[512,2048]{1,0:T(8,128)(2,1)S(1)}, f32[8,512]{1,0:T(8,128)S(1)}) custom-call(s32[3]{0:T(128)S(1)} %pad_add_fusion.place, f32[520,512]{1,0:T(8,128)S(1)} %select_select_fusion.pivot_ref, f32[4096,2048]{1,0:T(8,128)} %refs_0_.5, f32[512,2048]{1,0:T(8,128)} %collective-permute-done.14.refs_0_, ...), custom_call_target="tpu_custom_call" | custom-call | flops 6442450944 | bytes 8388608 | tf_op jit(solution)/shard_map/solve/pallas_call | solution.py:98
  421.4 11.4 %update.3 = (f32[4096,2048]{1,0:T(8,128)}, f32[1,4096]{1,0:T(1,128)}) custom-call(f32[4096,2048]{1,0:T(8,128)} %refs_0_.5, f32[1,4096]{1,0:T(1,128)S(1)} %bitcast.5, bf16[512,2048]{1,0:T(8,128)(2,1)S(1)} %get-tuple-element.49.refs_2_, bf16[512,2048]{1,0:T(8,128)(2,1)S(1)} %get-tuple-element.50.refs_3_, f32[8,512]{1,0:T(8,128)S(1)} %get-tuple-element.51.refs_4_, ...), custom_call_target="tpu_custom_call" | custom-call | flops 6442450944 | bytes 16777216 | tf_op jit(solution)/shard_map/update/pallas_call | solution.py:121
  432.8 18.7 %update.4 = (f32[4096,2048]{1,0:T(8,128)}, f32[1,4096]{1,0:T(1,128)}) custom-call(f32[4096,2048]{1,0:T(8,128)} %refs_0_.5, f32[1,4096]{1,0:T(1,128)S(1)} %bitcast.6, bf16[512,2048]{1,0:T(8,128)(2,1)S(1)} %get-tuple-element.49.refs_2_, bf16[512,2048]{1,0:T(8,128)(2,1)S(1)} %get-tuple-element.50.refs_3_, ...), custom_call_target="tpu_custom_call", output_to_operand_aliasing={{0}: (9, {}), {1}: (10, {})} | custom-call | flops 12884901888 | bytes 33554432 | tf_op jit(solution)/shard_map/update/pallas_call | solution.py:121
  451.5 11.4 %update.5 = (f32[4096,2048]{1,0:T(8,128)}, f32[1,4096]{1,0:T(1,128)}) custom-call(f32[4096,2048]{1,0:T(8,128)} %refs_0_.5, f32[1,4096]{1,0:T(1,128)S(1)} %bitcast.7, bf16[512,2048]{1,0:T(8,128)(2,1)S(1)} %get-tuple-element.49.refs_2_, bf16[512,2048]{1,0:T(8,128)(2,1)S(1)} %get-tuple-element.50.refs_3_, ...), custom_call_target="tpu_custom_call", output_to_operand_aliasing={{0}: (7, {}), {1}: (8, {})} | custom-call | flops 6442450944 | bytes 16777216 | tf_op jit(solution)/shard_map/update/pallas_call | solution.py:121
  (252 shorter events, 97.1 us)
Async XLA Ops:
  5.8 25.7 %collective-permute-start.37 = (f32[256,512]{1,0:T(8,128)S(1)}, f32[256,512]{1,0:T(8,128)S(1)}, u32[]{:S(2)}, u32[]{:S(2)}) collective-permute-start(f32[256,512]{1,0:T(8,128)S(1)} %get-tuple-element.42), channel_id=1, source_target_pairs={{0,1},{8,9},{16,17},{24,25}} | collective-permute-start | bytes 1572872 | tf_op jit(solution)/shard_map/ppermute | solution.py:194
  8.8 33.9 %collective-permute-start.43 = (f32[256,512]{1,0:T(8,128)S(1)}, f32[256,512]{1,0:T(8,128)S(1)}, u32[]{:S(2)}, u32[]{:S(2)}) collective-permute-start(f32[256,512]{1,0:T(8,128)S(1)} %get-tuple-element.44), channel_id=1, source_target_pairs={{0,1},{8,9},{16,17},{24,25}} | collective-permute-start | bytes 1572872 | tf_op jit(solution)/shard_map/ppermute | solution.py:194
  10.1 33.9 %collective-permute-start.36 = (f32[256,512]{1,0:T(8,128)S(1)}, f32[256,512]{1,0:T(8,128)S(1)}, u32[]{:S(2)}, u32[]{:S(2)}) collective-permute-start(f32[256,512]{1,0:T(8,128)S(1)} %get-tuple-element.45), channel_id=1, source_target_pairs={{0,4},{8,12},{16,20},{24,28}} | collective-permute-start | bytes 1572872 | tf_op jit(solution)/shard_map/ppermute | solution.py:194
  20.2 33.7 %collective-permute-start.50 = (f32[256,512]{1,0:T(8,128)S(1)}, f32[256,512]{1,0:T(8,128)S(1)}, u32[]{:S(2)}, u32[]{:S(2)}) collective-permute-start(f32[256,512]{1,0:T(8,128)S(1)} %get-tuple-element.46), channel_id=1, source_target_pairs={{0,1},{8,9},{16,17},{24,25}} | collective-permute-start | bytes 1572872 | tf_op jit(solution)/shard_map/ppermute | solution.py:194
  21.5 33.1 %collective-permute-start.44 = (f32[256,512]{1,0:T(8,128)S(1)}, f32[256,512]{1,0:T(8,128)S(1)}, u32[]{:S(2)}, u32[]{:S(2)}) collective-permute-start(f32[256,512]{1,0:T(8,128)S(1)} %get-tuple-element.47), channel_id=1, source_target_pairs={{0,4},{8,12},{16,20},{24,28}} | collective-permute-start | bytes 1572872 | tf_op jit(solution)/shard_map/ppermute | solution.py:194
  44.0 32.4 %collective-permute-start.24 = (f32[256,512]{1,0:T(8,128)S(1)}, f32[256,512]{1,0:T(8,128)S(1)}, u32[]{:S(2)}, u32[]{:S(2)}) collective-permute-start(f32[256,512]{1,0:T(8,128)S(1)} %get-tuple-element.56), channel_id=1, source_target_pairs={{0,1},{8,9},{16,17},{24,25}} | collective-permute-start | bytes 1572872 | tf_op jit(solution)/shard_map/ppermute | solution.py:194
  54.6 33.0 %collective-permute-start.31 = (f32[256,512]{1,0:T(8,128)S(1)}, f32[256,512]{1,0:T(8,128)S(1)}, u32[]{:S(2)}, u32[]{:S(2)}) collective-permute-start(f32[256,512]{1,0:T(8,128)S(1)} %get-tuple-element.59), channel_id=1, source_target_pairs={{0,1},{8,9},{16,17},{24,25}} | collective-permute-start | bytes 1572872 | tf_op jit(solution)/shard_map/ppermute | solution.py:194
  56.0 33.2 %collective-permute-start.51 = (f32[256,512]{1,0:T(8,128)S(1)}, f32[256,512]{1,0:T(8,128)S(1)}, u32[]{:S(2)}, u32[]{:S(2)}) collective-permute-start(f32[256,512]{1,0:T(8,128)S(1)} %get-tuple-element.62), channel_id=1, source_target_pairs={{0,4},{8,12},{16,20},{24,28}} | collective-permute-start | bytes 1572872 | tf_op jit(solution)/shard_map/ppermute | solution.py:194
  65.2 33.7 %collective-permute-start.57 = (f32[256,512]{1,0:T(8,128)S(1)}, f32[256,512]{1,0:T(8,128)S(1)}, u32[]{:S(2)}, u32[]{:S(2)}) collective-permute-start(f32[256,512]{1,0:T(8,128)S(1)} %get-tuple-element.64), channel_id=1, source_target_pairs={{0,1},{8,9},{16,17},{24,25}} | collective-permute-start | bytes 1572872 | tf_op jit(solution)/shard_map/ppermute | solution.py:194
  76.4 24.6 %collective-permute-start.58 = (f32[256,512]{1,0:T(8,128)S(1)}, f32[256,512]{1,0:T(8,128)S(1)}, u32[]{:S(2)}, u32[]{:S(2)}) collective-permute-start(f32[256,512]{1,0:T(8,128)S(1)} %get-tuple-element.65), channel_id=1, source_target_pairs={{0,4},{8,12},{16,20},{24,28}} | collective-permute-start | bytes 1572872 | tf_op jit(solution)/shard_map/ppermute | solution.py:194
  77.1 26.1 %collective-permute-start.2 = (f32[256,512]{1,0:T(8,128)}, f32[256,512]{1,0:T(8,128)}, u32[]{:S(2)}, u32[]{:S(2)}) collective-permute-start(f32[256,512]{1,0:T(8,128)} %collective-permute-done), channel_id=1, source_target_pairs={{4,2},{12,10},{20,18},{28,26}} | collective-permute-start | bytes 1572872 | tf_op jit(solution)/shard_map/ppermute | solution.py:194
  103.2 170.1 %collective-permute-start.15 = (f32[512,2048]{1,0:T(8,128)}, f32[512,2048]{1,0:T(8,128)}, u32[]{:S(2)}, u32[]{:S(2)}) collective-permute-start(f32[512,2048]{1,0:T(8,128)} %slice.137), channel_id=1, source_target_pairs={{0,16},{1,17},{2,18},{3,19},{4,20},{5,21},{6,22},{7,23}} | collective-permute-start | bytes 12582920 | tf_op jit(solution)/shard_map/ppermute | solution.py:199
  106.1 28.3 %collective-permute-start.52 = (f32[256,512]{1,0:T(8,128)S(1)}, f32[256,512]{1,0:T(8,128)S(1)}, u32[]{:S(2)}, u32[]{:S(2)}) collective-permute-start(f32[256,512]{1,0:T(8,128)S(1)} %collective-permute-done.50), channel_id=1, source_target_pairs={{1,5},{9,13},{17,21},{25,29}} | collective-permute-start | bytes 1572872 | tf_op jit(solution)/shard_map/ppermute | solution.py:194
  108.7 36.9 %collective-permute-start.19 = (f32[256,512]{1,0:T(8,128)S(1)}, f32[256,512]{1,0:T(8,128)S(1)}, u32[]{:S(2)}, u32[]{:S(2)}) collective-permute-start(f32[256,512]{1,0:T(8,128)S(1)} %collective-permute-done.18), channel_id=1, source_target_pairs={{1,5},{9,13},{17,21},{25,29}} | collective-permute-start | bytes 1572872 | tf_op jit(solution)/shard_map/ppermute | solution.py:194
  111.9 44.9 %collective-permute-start.26 = (f32[256,512]{1,0:T(8,128)S(1)}, f32[256,512]{1,0:T(8,128)S(1)}, u32[]{:S(2)}, u32[]{:S(2)}) collective-permute-start(f32[256,512]{1,0:T(8,128)S(1)} %collective-permute-done.24), channel_id=1, source_target_pairs={{1,5},{9,13},{17,21},{25,29}} | collective-permute-start | bytes 1572872 | tf_op jit(solution)/shard_map/ppermute | solution.py:194
  123.1 44.9 %collective-permute-start.32 = (f32[256,512]{1,0:T(8,128)S(1)}, f32[256,512]{1,0:T(8,128)S(1)}, u32[]{:S(2)}, u32[]{:S(2)}) collective-permute-start(f32[256,512]{1,0:T(8,128)S(1)} %copy-done.27), channel_id=1, source_target_pairs={{1,5},{9,13},{17,21},{25,29}} | collective-permute-start | bytes 1572872 | tf_op jit(solution)/shard_map/ppermute | solution.py:194
  134.4 44.9 %collective-permute-start.59 = (f32[256,512]{1,0:T(8,128)S(1)}, f32[256,512]{1,0:T(8,128)S(1)}, u32[]{:S(2)}, u32[]{:S(2)}) collective-permute-start(f32[256,512]{1,0:T(8,128)S(1)} %copy-done.24), channel_id=1, source_target_pairs={{1,5},{9,13},{17,21},{25,29}} | collective-permute-start | bytes 1572872 | tf_op jit(solution)/shard_map/ppermute | solution.py:194
  145.6 35.4 %collective-permute-start.9 = (f32[256,512]{1,0:T(8,128)S(1)}, f32[256,512]{1,0:T(8,128)S(1)}, u32[]{:S(2)}, u32[]{:S(2)}) collective-permute-start(f32[256,512]{1,0:T(8,128)S(1)} %broadcast_select_fusion.6), channel_id=1, source_target_pairs={{4,2},{5,3},{12,10},{13,11},{20,18},{21,19},{28,26},{29,27}} | collective-permute-start | bytes 1572872 | tf_op jit(solution)/shard_map/ppermute | solution.py:194
  156.8 24.8 %collective-permute-start.8 = (f32[256,512]{1,0:T(8,128)S(1)}, f32[256,512]{1,0:T(8,128)S(1)}, u32[]{:S(2)}, u32[]{:S(2)}) collective-permute-start(f32[256,512]{1,0:T(8,128)S(1)} %broadcast_select_fusion.6), channel_id=1, source_target_pairs={{4,6},{5,7},{12,14},{13,15},{20,22},{21,23},{28,30},{29,31}} | collective-permute-start | bytes 1572872 | tf_op jit(solution)/shard_map/ppermute | solution.py:194
  190.5 72.5 %collective-permute-start.10 = (f32[256,512]{1,0:T(8,128)S(1)}, f32[256,512]{1,0:T(8,128)S(1)}, u32[]{:S(2)}, u32[]{:S(2)}) collective-permute-start(f32[256,512]{1,0:T(8,128)S(1)} %select_select_fusion.24), channel_id=1, source_target_pairs={{2,3},{3,2},{4,5},{5,4},{6,7},{7,6},{10,11},{11,10},{12,13},{13,12... | collective-permute-start | bytes 1572872 | tf_op jit(solution)/shard_map/ppermute | solution.py:194
  191.2 70.3 %collective-permute-start.4 = (f32[256,512]{1,0:T(8,128)S(1)}, f32[256,512]{1,0:T(8,128)S(1)}, u32[]{:S(2)}, u32[]{:S(2)}) collective-permute-start(f32[256,512]{1,0:T(8,128)S(1)} %collective-permute-done.3), channel_id=1, source_target_pairs={{3,1},{11,9},{19,17},{27,25}} | collective-permute-start | bytes 1572872 | tf_op jit(solution)/shard_map/ppermute | solution.py:194
  192.7 71.1 %collective-permute-start.41 = (f32[256,512]{1,0:T(8,128)S(1)}, f32[256,512]{1,0:T(8,128)S(1)}, u32[]{:S(2)}, u32[]{:S(2)}) collective-permute-start(f32[256,512]{1,0:T(8,128)S(1)} %select_select_fusion.14), channel_id=1, source_target_pairs={{2,3},{3,2},{4,5},{5,4},{6,7},{7,6},{10,11},{11,10},{12,13},{13,12... | collective-permute-start | bytes 1572872 | tf_op jit(solution)/shard_map/ppermute | solution.py:194
  193.6 71.1 %collective-permute-start.48 = (f32[256,512]{1,0:T(8,128)S(1)}, f32[256,512]{1,0:T(8,128)}, u32[]{:S(2)}, u32[]{:S(2)}) collective-permute-start(f32[256,512]{1,0:T(8,128)S(1)} %select_select_fusion.13), channel_id=1, source_target_pairs={{2,3},{3,2},{4,5},{5,4},{6,7},{7,6},{10,11},{11,10},{12,13},{13,12... | collective-permute-start | bytes 1572872 | tf_op jit(solution)/shard_map/ppermute | solution.py:194
  265.4 39.6 %collective-permute-start.64 = (f32[256,512]{1,0:T(8,128)S(1)}, f32[256,512]{1,0:T(8,128)S(1)}, u32[]{:S(2)}, u32[]{:S(2)}) collective-permute-start(f32[256,512]{1,0:T(8,128)S(1)} %collective-permute-done.10), channel_id=1, source_target_pairs={{3,1},{11,9},{19,17},{27,25}} | collective-permute-start | bytes 1572872 | tf_op jit(solution)/shard_map/ppermute | solution.py:194
  266.7 50.8 %collective-permute-start.42 = (f32[256,512]{1,0:T(8,128)S(1)}, f32[256,512]{1,0:T(8,128)S(1)}, u32[]{:S(2)}, u32[]{:S(2)}) collective-permute-start(f32[256,512]{1,0:T(8,128)S(1)} %collective-permute-done.41), channel_id=1, source_target_pairs={{3,1},{11,9},{19,17},{27,25}} | collective-permute-start | bytes 1572872 | tf_op jit(solution)/shard_map/ppermute | solution.py:194
  268.1 144.0 %collective-permute-start.14 = (f32[512,2048]{1,0:T(8,128)}, f32[512,2048]{1,0:T(8,128)}, u32[]{:S(2)}, u32[]{:S(2)}) collective-permute-start(f32[512,2048]{1,0:T(8,128)} %slice.137), channel_id=1, source_target_pairs={{0,8},{8,0},{16,24},{24,16},{1,9},{9,1},{17,25},{25,17},{2,10},{10... | collective-permute-start | bytes 12582920 | tf_op jit(solution)/shard_map/ppermute | solution.py:200
  273.3 138.8 %collective-permute-start.16 = (f32[512,2048]{1,0:T(8,128)}, f32[512,2048]{1,0:T(8,128)}, u32[]{:S(2)}, u32[]{:S(2)}) collective-permute-start(f32[512,2048]{1,0:T(8,128)} %collective-permute-done.15.refs_1_), channel_id=1, source_target_pairs={{0,8},{8,0},{16,24},{24,16},{1,9},{9,1},{17,25},{25,17},{2,10},{10... | collective-permute-start | bytes 12582920 | tf_op jit(solution)/shard_map/ppermute | solution.py:200
  273.4 68.0 %collective-permute-start.49 = (f32[256,512]{1,0:T(8,128)}, f32[256,512]{1,0:T(8,128)}, u32[]{:S(2)}, u32[]{:S(2)}) collective-permute-start(f32[256,512]{1,0:T(8,128)} %collective-permute-done.48), channel_id=1, source_target_pairs={{3,1},{11,9},{19,17},{27,25}} | collective-permute-start | bytes 1572872 | tf_op jit(solution)/shard_map/ppermute | solution.py:194
  305.0 47.5 %collective-permute-start.23 = (f32[256,512]{1,0:T(8,128)}, f32[256,512]{1,0:T(8,128)}, u32[]{:S(2)}, u32[]{:S(2)}) collective-permute-start(f32[256,512]{1,0:T(8,128)} %collective-permute-done.22), channel_id=1, source_target_pairs={{3,1},{11,9},{19,17},{27,25}} | collective-permute-start | bytes 1572872 | tf_op jit(solution)/shard_map/ppermute | solution.py:194
  318.4 45.5 %collective-permute-start.30 = (f32[256,512]{1,0:T(8,128)S(1)}, f32[256,512]{1,0:T(8,128)}, u32[]{:S(2)}, u32[]{:S(2)}) collective-permute-start(f32[256,512]{1,0:T(8,128)S(1)} %collective-permute-done.29), channel_id=1, source_target_pairs={{3,1},{11,9},{19,17},{27,25}} | collective-permute-start | bytes 1572872 | tf_op jit(solution)/shard_map/ppermute | solution.py:194
  341.4 45.6 %collective-permute-start.35 = (f32[256,512]{1,0:T(8,128)S(1)}, f32[256,512]{1,0:T(8,128)S(1)}, u32[]{:S(2)}, u32[]{:S(2)}) collective-permute-start(f32[256,512]{1,0:T(8,128)S(1)} %select_select_fusion.17), channel_id=1, source_target_pairs={{3,2},{5,4},{7,6},{11,10},{13,12},{15,14},{19,18},{21,20},{23,22},... | collective-permute-start | bytes 1572872 | tf_op jit(solution)/shard_map/ppermute | solution.py:194
  375.0 36.6 %collective-permute-start.13 = (f32[520,512]{1,0:T(8,128)S(1)}, f32[520,512]{1,0:T(8,128)S(1)}, u32[]{:S(2)}, u32[]{:S(2)}) collective-permute-start(f32[520,512]{1,0:T(8,128)S(1)} %pad_maximum_fusion), channel_id=1, source_target_pairs={{0,8},{8,0},{16,24},{24,16},{1,9},{9,1},{17,25},{25,17},{2,10},{10... | collective-permute-start | bytes 3194888 | tf_op jit(solution)/shard_map/ppermute | solution.py:200
  (91 other events, 1829.4 us)
